TPU v7x, 32 devices: a whole 2x2x4 slice. The times are simulated.
32 devices in a mesh: groups: 2 (over y), span: 4 (over z), batch: 4 (over x, core).
Axes of the slice: x: 2, y: 2, z: 4, core: 2. Of those that a mesh axis runs over, the one named last changes fastest.
Arguments:
- embeddings: bfloat16 [8, 512, 768], P(('groups', 'batch'), 'span'), parts along dimension 0, may hold values from -3500 to 3500
- cluster_ids: int32 [8, 512], P(('groups', 'batch'), 'span'), parts along dimension 0, may hold values from 0 to 15, as said below
Outputs:
- nearest: float32 [8, 512], P(('groups', 'batch'), 'span'), parts along dimension 0
There are 2 independent parts, one for each index of `groups`. A program takes and returns all parts, laid end to end along the dimension named above; each array names one. Nothing has to cross between parts.
Inputs may be any that keep to these rules, and one draw needn't show every extreme that they name: `cluster_ids`: on one device at most 96 rows carry ids of one residue modulo 4; in every batch some residue has exactly 96 rows on every device of the span.
All inputs are finite; a program needn't handle non-finite values.
Results may differ from a plain program's by a relative error of at most 0.00061.
Values may be sent and summed in bfloat16 or wider, within the bound.
No kernel may reach another device: no remote copies, remote signals or barrier semaphores. Data moves between devices by JAX's collectives and lax.ppermute only.
A program may use at most 64 MiB of HBM per device.

v0:
```python
import math
import jax
import jax.numpy as jnp
from jax import lax
from jax.sharding import PartitionSpec as P


def normalize(embeddings):
    values = embeddings.astype(jnp.float32)
    inverse = lax.rsqrt(jnp.mean(values * values, axis=-1, keepdims=True) + 1e-06)
    return (values * inverse * (1.0 / math.sqrt(values.shape[-1]))).astype(jnp.bfloat16)


def pair_scores(left, right):
    return lax.dot_general(
        left, right, (((1,), (1,)), ((), ())), preferred_element_type=jnp.float32
    )


def per_device(embeddings, cluster_ids):
    normed = normalize(embeddings[0])
    member_ids = cluster_ids[0]
    row_count = normed.shape[0]
    own_index = lax.axis_index("span")
    own_rows = own_index * row_count + jnp.arange(row_count, dtype=jnp.int32)
    start_value = jnp.full((row_count,), -1.0, jnp.float32)
    piece_rows = lax.all_gather(normed, "span", axis=0, tiled=True)
    piece_ids = lax.all_gather(member_ids.astype(jnp.bfloat16), "span", axis=0, tiled=True)
    scores = pair_scores(normed, piece_rows)
    column_rows = jnp.arange(piece_rows.shape[0], dtype=jnp.int32)
    same_cluster = (member_ids[:, None] == piece_ids.astype(jnp.int32)[None, :]) & (
        own_rows[:, None] != column_rows[None, :]
    )
    nearest = jnp.maximum(start_value, jnp.max(jnp.where(same_cluster, scores, -1.0), axis=1))
    return nearest[None, :]


def solution(mesh):
    return jax.shard_map(
        per_device,
        mesh=mesh,
        in_specs=(P(("groups", "batch"), "span", None), P(("groups", "batch"), "span")),
        out_specs=P(("groups", "batch"), "span"),
        check_vma=False,
    )
```

profile of v0, /device:TPU:0, one launch (start us, length us, event | category | flops | bytes accessed | tf_op | source)
XLA Modules:
  0.0 32.1 jit_solution(1568791861424258728)
XLA Ops:
  0.0 0.0 copy-start
  0.0 1.1 %fusion.1 = f32[128]{0:T(128)S(1)} fusion(bf16[1,128,768]{2,1,0:T(8,128)(2,1)} %param.2), kind=kLoop, calls=%fused_computation.4 | loop fusion | flops 294784 | bytes 197120 | tf_op jit(solution)/shard_map/reduce_sum | solution.py:10
  1.1 0.0 copy-start.1
  1.1 0.6 %copy-done.1 = s32[1,128]{1,0:T(1,128)S(1)} copy-done((s32[1,128]{1,0:T(1,128)S(1)}, s32[1,128]{1,0:T(1,128)}, u32[]{:S(2)}) %copy-start.1) | copy-done | bytes 536
  1.8 12.6 %all-gather = bf16[4,1,128]{2,1,0:T(2,128)(2,1)S(1)} all-gather(bf16[1,1,128]{2,1,0:T(2,128)(2,1)S(1)} %convert_bitcast_fusion), channel_id=1, replica_groups=mesh['groups'=2,'span'=4,'batch'=4] {'span'}, dimensions={0}, use_global_device_ids=true | all-gather | bytes 1280 | tf_op jit(solution)/shard_map/all_gather | solution.py:28
  14.4 0.0 copy-done
  14.4 0.1 fusion.3
  14.5 16.6 %all_gather.7 = bf16[512,768]{1,0:T(8,128)(2,1)S(1)} all-gather(bf16[128,768]{1,0:T(8,128)(2,1)S(1)} %fusion.3), channel_id=1, replica_groups=mesh['groups'=2,'span'=4,'batch'=4] {'span'}, dimensions={0}, use_global_device_ids=true | all-gather | bytes 983040 | tf_op jit(solution)/shard_map/all_gather | solution.py:27
  31.1 0.5 %fusion = f32[128]{0:T(128)S(1)} fusion(bf16[128,768]{1,0:T(8,128)(2,1)S(1)} %fusion.3, bf16[512,768]{1,0:T(8,128)(2,1)S(1)} %all_gather.7, s32[128]{0:T(128)S(1)} %iota_add_fusion, s32[512]{0:T(512)S(1)} %bitcast.13, s32[128]{0:T(128)S(1)} %bitcast.14), kind=kOutput, calls=%fused_computation.1 | convolution fusion | flops 100990848 | bytes 986624 | tf_op jit(solution)/shard_map/dot_general | solution.py:15
  31.6 0.5 %maximum_bitcast_fusion = f32[1,128]{1,0:T(1,128)} fusion(f32[128]{0:T(128)S(1)} %fusion), kind=kLoop, calls=%fused_computation.9 | loop fusion | flops 128 | bytes 1024 | tf_op jit(solution)/shard_map/max;broadcast_in_dim | solution.py:34
  (4 shorter events, 0.0 us)
Async XLA Ops:
  0.0 14.4 %copy-start = (bf16[1,128,768]{2,1,0:T(8,128)(2,1)S(1)}, bf16[1,128,768]{2,1,0:T(8,128)(2,1)}, u32[]{:S(2)}) copy-start(bf16[1,128,768]{2,1,0:T(8,128)(2,1)} %param.2) | copy-start | bytes 589828
  1.1 0.7 %copy-start.1 = (s32[1,128]{1,0:T(1,128)S(1)}, s32[1,128]{1,0:T(1,128)}, u32[]{:S(2)}) copy-start(s32[1,128]{1,0:T(1,128)} %param.3) | copy-start | bytes 1540
where the time goes:
time: 32.3 us; the launch traced here: 32.1 us
  blocking collectives  29.2 us (90%)
  other arithmetic  1.77 us (5%)
  local copies, waits for them, and re-layouts  0.65 us (2%)
  matrix products  0.47 us (1%)
    all_gather x1, blocking collectives, per_device(): piece_rows = lax.all_gather(normed, 'span', axis=0, tiled=True)  16.6 us
    all_gather x1, blocking collectives, per_device(): lax.all_gather(member_ids.astype(jnp.bfloat16), 'span', axis=0, tiled=True)  12.6 us
    reduce_sum x1, other arithmetic, normalize(): jnp.mean(values * values, axis=-1, keepdims=True) + 1e-06  1.11 us

commit v1 on v0

--- a/solution.py
+++ b/solution.py
@@ -25,7 +25,11 @@
     own_rows = own_index * row_count + jnp.arange(row_count, dtype=jnp.int32)
     start_value = jnp.full((row_count,), -1.0, jnp.float32)
     piece_rows = lax.all_gather(normed, "span", axis=0, tiled=True)
-    piece_ids = lax.all_gather(member_ids.astype(jnp.bfloat16), "span", axis=0, tiled=True)
+    block = member_ids.astype(jnp.bfloat16)
+    size = lax.axis_size("span")
+    blocks = jnp.stack([block for _ in range(size)])
+    blocks = lax.all_to_all(blocks, "span", split_axis=0, concat_axis=0)
+    piece_ids = jnp.concatenate(blocks, axis=0)
     scores = pair_scores(normed, piece_rows)
     column_rows = jnp.arange(piece_rows.shape[0], dtype=jnp.int32)
     same_cluster = (member_ids[:, None] == piece_ids.astype(jnp.int32)[None, :]) & (

time: 32.3 us -> 30.8 us (0.954)
  blocking collectives: 29.2 us -> 20.1 us
  starting transfers between devices: 0 us -> 6.35 us
  other arithmetic: 1.77 us -> 2.4 us
  local copies, waits for them, and re-layouts: 0.65 us -> 1.25 us
    all_gather x1 -> x0, blocking collectives: 12.6 us -> none  [per_device(): lax.all_gather(member_ids.astype(jnp.bfloat16), 'span', axis=0, tiled=True)]
    all_to_all x0 -> x1, starting transfers between devices: none -> 6.35 us  [per_device(): blocks = lax.all_to_all(blocks, 'span', split_axis=0, concat_axis=0)]
    all_gather x1, blocking collectives: 16.6 us -> 20.1 us  [per_device(): piece_rows = lax.all_gather(normed, 'span', axis=0, tiled=True)]
    convert_element_type x0 -> x1, other arithmetic: none -> 0.7 us  [per_device(): block = member_ids.astype(jnp.bfloat16)]
    another operation x0 -> x1, local copies, waits for them, and re-layouts: none -> 0.6 us  [per_device(): blocks = jnp.stack([block for _ in range(size)])]
  transfers between devices with their start and end apart: 0 -> 1, of which waited for: 0 -> 0; matrix products, arithmetic and copies ran while one was open for 0% -> 4% of each run, Pallas kernels for 0% -> 0%
where the time goes in v1:
time: 30.8 us; the launch traced here: 30.6 us
  blocking collectives  20.1 us (65%)
  starting transfers between devices  6.35 us (21%)
  other arithmetic  2.4 us (8%)
  local copies, waits for them, and re-layouts  1.25 us (4%)
  matrix products  0.47 us (2%)
    all_gather x1, blocking collectives, per_device(): piece_rows = lax.all_gather(normed, 'span', axis=0, tiled=True)  20.1 us
    all_to_all x1, starting transfers between devices, per_device(): blocks = lax.all_to_all(blocks, 'span', split_axis=0, concat_axis=0)  6.35 us
    reduce_sum x1, other arithmetic, normalize(): jnp.mean(values * values, axis=-1, keepdims=True) + 1e-06  1.05 us
    convert_element_type x1, other arithmetic, per_device(): block = member_ids.astype(jnp.bfloat16)  0.7 us
    unnamed x4, local copies, waits for them, and re-layouts  0.65 us
  transfers between devices with their start and end apart: 1, of which 0 were waited for; matrix products, arithmetic and copies ran while one was open for 4% of the time, Pallas kernels for 0%

profile of v1, /device:TPU:0, one launch (start us, length us, event | category | flops | bytes accessed | tf_op | source)
XLA Modules:
  0.0 30.6 jit_solution(15222487123422209843)
XLA Ops:
  0.0 0.0 copy-start
  0.0 0.7 %convert_bitcast_fusion = bf16[128]{0:T(256)(128)(2,1)S(1)} fusion(s32[1,128]{1,0:T(1,128)} %param.3), kind=kLoop, calls=%fused_computation.12 | loop fusion | flops 128 | bytes 768 | tf_op jit(solution)/shard_map/convert_element_type | solution.py:28
  0.7 0.6 %stack.2 = bf16[4,1,128]{2,1,0:T(2,128)(2,1)} broadcast(bf16[128]{0:T(256)(128)(2,1)S(1)} %convert_bitcast_fusion), dimensions={2} | broadcast | bytes 1280 | tf_op jit(solution)/shard_map/stack | solution.py:30
  1.3 6.3 %all-to-all-start = ((bf16[4,1,128]{2,1,0:T(2,128)(2,1)}), bf16[4,1,128]{2,1,0:T(2,128)(2,1)S(1)}, u32[]{:S(2)}, u32[]{:S(2)}) async-start(bf16[4,1,128]{2,1,0:T(2,128)(2,1)} %stack.2), calls=%async_computation | async-start | bytes 4096 | tf_op jit(solution)/shard_map/all_to_all | solution.py:31
  7.6 1.0 %fusion.1 = f32[128]{0:T(128)S(1)} fusion(bf16[1,128,768]{2,1,0:T(8,128)(2,1)} %param.2), kind=kLoop, calls=%fused_computation.4 | loop fusion | flops 294784 | bytes 197120 | tf_op jit(solution)/shard_map/reduce_sum | solution.py:10
  8.7 0.0 copy-done
  8.7 0.1 fusion.3
  8.8 20.1 %all_gather.3 = bf16[512,768]{1,0:T(8,128)(2,1)S(1)} all-gather(bf16[128,768]{1,0:T(8,128)(2,1)S(1)} %fusion.3), channel_id=1, replica_groups=mesh['groups'=2,'span'=4,'batch'=4] {'span'}, dimensions={0}, use_global_device_ids=true | all-gather | bytes 983040 | tf_op jit(solution)/shard_map/all_gather | solution.py:27
  28.9 0.0 all-to-all-done
  28.9 0.0 copy-start.1
  28.9 0.6 %copy-done.1 = s32[1,128]{1,0:T(1,128)S(1)} copy-done((s32[1,128]{1,0:T(1,128)S(1)}, s32[1,128]{1,0:T(1,128)}, u32[]{:S(2)}) %copy-start.1) | copy-done | bytes 536
  29.6 0.5 %fusion = f32[128]{0:T(128)S(1)} fusion(bf16[128,768]{1,0:T(8,128)(2,1)S(1)} %fusion.3, bf16[512,768]{1,0:T(8,128)(2,1)S(1)} %all_gather.3, s32[128]{0:T(128)S(1)} %iota_add_fusion, s32[512]{0:T(512)S(1)} %bitcast.12, s32[128]{0:T(128)S(1)} %bitcast.13), kind=kOutput, calls=%fused_computation.1 | convolution fusion | flops 100990848 | bytes 986624 | tf_op jit(solution)/shard_map/dot_general | solution.py:15
  30.0 0.5 %maximum_bitcast_fusion = f32[1,128]{1,0:T(1,128)} fusion(f32[128]{0:T(128)S(1)} %fusion), kind=kLoop, calls=%fused_computation.9 | loop fusion | flops 128 | bytes 1024 | tf_op jit(solution)/shard_map/max;broadcast_in_dim | solution.py:38
  (3 shorter events, 0.0 us)
Async XLA Ops:
  0.0 8.7 %copy-start = (bf16[1,128,768]{2,1,0:T(8,128)(2,1)S(1)}, bf16[1,128,768]{2,1,0:T(8,128)(2,1)}, u32[]{:S(2)}) copy-start(bf16[1,128,768]{2,1,0:T(8,128)(2,1)} %param.2) | copy-start | bytes 589828
  1.3 27.6 %all-to-all-start = ((bf16[4,1,128]{2,1,0:T(2,128)(2,1)}), bf16[4,1,128]{2,1,0:T(2,128)(2,1)S(1)}, u32[]{:S(2)}, u32[]{:S(2)}) async-start(bf16[4,1,128]{2,1,0:T(2,128)(2,1)} %stack.2), calls=%async_computation | async-start | bytes 4096 | tf_op jit(solution)/shard_map/all_to_all | solution.py:31
  28.9 0.7 %copy-start.1 = (s32[1,128]{1,0:T(1,128)S(1)}, s32[1,128]{1,0:T(1,128)}, u32[]{:S(2)}) copy-start(s32[1,128]{1,0:T(1,128)} %param.3) | copy-start | bytes 1540
